TPU v7x, 32 devices: a whole 2x2x4 slice. The times are simulated.
32 devices in a mesh: seq: 4 (over z), phase: 4 (over y, x), dp: 2 (over core).
Axes of the slice: x: 2, y: 2, z: 4, core: 2. Of those that a mesh axis runs over, the one named last changes fastest.
Arguments:
- byte_embed: bfloat16 [4096, 1536], P(('dp', 'seq')), parts along dimension 0, may hold values from -6 to 6
- in_gain: float32 [1536], replicated, may hold values from 0.25 to 1.75
- w_qkv: bfloat16 [1536, 3, 1536], P('seq', None, 'phase')
- w_up: bfloat16 [1536, 3072], P('phase')
- out_gain: float32 [3072], P('phase'), may hold values from 0.25 to 1.75
- bounds: int32 [1024], P(('dp', 'seq')), parts along dimension 0, may hold values from 0 to 2047, as said below
- owner: int32 [1024, 1], P(('dp', 'seq')), parts along dimension 0, may hold values from 0 to 3; in each aligned block of 128 rows (0 to 127, 128 to 255, ...) at most 64 rows name the same one
Outputs:
- byte_states: bfloat16 [4096, 1536], P(('dp', 'seq'), 'phase'), parts along dimension 0
- stretch_states: bfloat16 [2048, 3072], P(('dp', 'seq'), 'phase'), parts along dimension 0
There are 2 independent parts, one for each index of `dp`. A program takes and returns all parts, laid end to end along the dimension named above; an argument that names none is the same for every part. Nothing has to cross between parts.
Inputs may be any that keep to these rules, and one draw needn't show every extreme that they name: `bounds`: strictly rising; the 128 entries of block b lie in bytes b * 512 to (b + 1) * 512 - 1, and the first and last byte of each block are among them. Among the 128 stretch rows of one block no owner is named more than 64 times.
All inputs are finite; a program needn't handle non-finite values.
Results may differ from a plain program's by a relative error of at most 0.013.
Values may be sent and summed in bfloat16 or wider, within the bound.
A program may use at most 128 MiB of HBM per device.

v0:
```python
import jax
import jax.numpy as jnp
from jax import lax
from jax.sharding import PartitionSpec as P

DC = 3072
HD = 128
WINDOW = 1024


def passed_along(value, axis, by):
    devices = lax.axis_size(axis)
    pairs = [(i, i + by) for i in range(devices) if 0 <= i + by < devices]
    return lax.ppermute(value, axis, pairs)


def project_rows(rows, w_up, out_gain):
    groups = lax.axis_size("phase")
    full_rows = lax.all_gather(rows, "phase", axis=1, tiled=True)
    w_cols = lax.all_to_all(w_up, "phase", split_axis=1, concat_axis=0, tiled=True)
    count = full_rows.shape[0]
    width = rows.shape[1]
    columns = w_cols.shape[1]
    pieces = jnp.einsum(
        "nsg,sgc->snc",
        full_rows.reshape(count, groups, width),
        w_cols.reshape(groups, width, columns),
        preferred_element_type=jnp.float32,
    )
    projected = jnp.sum(pieces.astype(jnp.bfloat16).astype(jnp.float32), axis=0)
    squares = lax.psum(jnp.sum(projected * projected, axis=1), "phase")
    scale = lax.rsqrt(squares / DC + 1e-05)
    return (projected * scale[:, None] * out_gain).astype(jnp.bfloat16)


def on_device(byte_embed, in_gain, w_qkv, w_up, out_gain, bounds, owner):
    tok = byte_embed.shape[0]
    n_seq = lax.axis_size("seq")
    mine = lax.axis_index("seq")
    section = lax.axis_index("phase")
    width_dev = w_qkv.shape[2]
    heads_dev = width_dev // HD
    x32 = byte_embed.astype(jnp.float32)
    normed = (x32 * lax.rsqrt(jnp.mean(x32 * x32, axis=1, keepdims=True) + 1e-05) * in_gain).astype(
        jnp.bfloat16
    )
    piece = lax.all_gather(w_qkv, "seq", axis=0, tiled=True)
    qkv = jnp.dot(
        normed, piece.reshape(piece.shape[0], 3 * width_dev), preferred_element_type=jnp.float32
    ).astype(jnp.bfloat16)
    qkv = qkv.reshape(tok, 3, heads_dev, HD)
    query = qkv[:, 0]
    keys = qkv[:, 1]
    values = qkv[:, 2]
    reach = -(-WINDOW // tok)
    key_list = [keys]
    value_list = [values]
    for distance in range(1, reach + 1):
        earlier_keys, earlier_values = passed_along((keys, values), "seq", distance)
        key_list = [earlier_keys] + key_list
        value_list = [earlier_values] + value_list
    key_all = jnp.concatenate(key_list, axis=0)
    value_all = jnp.concatenate(value_list, axis=0)
    scores = jnp.einsum(
        "ihd,jhd->hij", query, key_all, preferred_element_type=jnp.float32
    ) * HD ** (-0.5)
    q_pos = mine * tok + jnp.arange(tok, dtype=jnp.int32)
    k_pos = mine * tok - reach * tok + jnp.arange((reach + 1) * tok, dtype=jnp.int32)
    keep = (
        (k_pos[None, :] <= q_pos[:, None])
        & (k_pos[None, :] > q_pos[:, None] - WINDOW)
        & (k_pos[None, :] >= 0)
    )
    scores = jnp.where(keep[None], scores, -jnp.inf)
    top = jnp.max(scores, axis=2, keepdims=True)
    expo = jnp.exp(scores - top)
    probs = (expo / jnp.sum(expo, axis=2, keepdims=True)).astype(jnp.bfloat16)
    attended = jnp.einsum(
        "hij,jhd->ihd", probs, value_all, preferred_element_type=jnp.float32
    ).astype(jnp.bfloat16)
    attended = attended.reshape(tok, width_dev)
    residual = lax.dynamic_slice_in_dim(x32, section * width_dev, width_dev, 1)
    byte_states = (residual + attended.astype(jnp.float32)).astype(jnp.bfloat16)
    local = bounds - mine * tok
    stretch_rows = jnp.take(byte_states, local, axis=0)
    owners = owner[:, 0]
    crows = owners.shape[0]
    slot_count = 2 * crows // n_seq
    place = jnp.arange(crows, dtype=jnp.int32)
    earlier = (owners[:, None] == owners[None, :]) & (place[None, :] < place[:, None])
    rank = jnp.sum(earlier.astype(jnp.int32), axis=1)
    target = owners * slot_count + rank
    placing = (target[None, :] == jnp.arange(n_seq * slot_count, dtype=jnp.int32)[:, None]).astype(
        jnp.bfloat16
    )
    outgoing = jnp.dot(placing, stretch_rows, preferred_element_type=jnp.float32).astype(
        jnp.bfloat16
    )
    outgoing = outgoing.reshape(n_seq, slot_count, width_dev)
    arrived = lax.all_to_all(outgoing, "seq", split_axis=0, concat_axis=0, tiled=True).reshape(
        n_seq * slot_count, width_dev
    )
    stretch_states = project_rows(arrived, w_up, out_gain)
    return (byte_states, stretch_states)


def solution(mesh):
    return jax.shard_map(
        on_device,
        mesh=mesh,
        in_specs=(
            P(("dp", "seq"), None),
            P(),
            P("seq", None, "phase"),
            P("phase", None),
            P("phase"),
            P(("dp", "seq")),
            P(("dp", "seq"), None),
        ),
        out_specs=(P(("dp", "seq"), "phase"), P(("dp", "seq"), "phase")),
        check_vma=False,
    )
```

profile of v0, /device:TPU:0, one launch (start us, length us, event | category | flops | bytes accessed | tf_op | source)
XLA Modules:
  0.0 220.7 jit_solution(122934458647829781)
XLA Ops:
  7.2 0.0 copy-start
  7.2 0.0 all-gather.2.cloned.1.call-start
  7.2 2.4 %copy.31 = bf16[384,3,384]{0,2,1:T(8,128)(2,1)} copy(bf16[384,3,384]{2,0,1:T(8,128)(2,1)} %param.9) | data formatting | bytes 1769472 | tf_op args[2]
  9.6 0.0 all-gather.2.cloned.1.call-update
  9.6 0.0 copy-done
  9.6 0.0 copy-start.4
  9.6 0.0 copy-start.6
  9.7 0.0 copy-start.5
  9.7 2.0 convert_element_type.44
  11.7 0.0 copy-done.4
  11.8 0.2 convert_reduce_fusion.1
  12.0 0.4 multiply_reduce_fusion
  12.4 69.8 %all-gather.2.cloned.1.call-done = bf16[1536,3,384]{0,2,1:T(8,128)(2,1)} async-done(((bf16[384,3,384]{0,2,1:T(8,128)(2,1)}), bf16[1536,3,384]{0,2,1:T(8,128)(2,1)}) %all-gather.2.cloned.1.call-update) | async-done | bytes 3538960 | tf_op jit(solution)/shard_map/all_gather | solution.py:47
  82.2 4.3 %convolution_convert_fusion = bf16[512,1152]{1,0:T(8,128)(2,1)S(1)} fusion(bf16[1536,1152]{0,1:T(8,128)(2,1)} %bitcast.36, f32[1536]{0:T(1024)S(1)} %copy-done.5, f32[512]{0:T(512)S(1)} %add_rsqrt_fusion, bf16[512,1536]{1,0:T(8,128)(2,1)S(1)} %copy-done), kind=kOutput, calls=%fused_computation.14 | convolution fusion | flops 1815674880 | bytes 6299648 | tf_op jit(solution)/shard_map/dot_general | solution.py:48
  86.5 0.6 copy.32
  87.1 0.0 copy-start.1
  87.1 0.9 slice_bitcast_fusion.2
  88.0 0.2 copy.42
  88.2 2.9 %collective-permute-start.2 = (bf16[512,3,128]{2,0,1:T(8,128)(2,1)S(1)}, bf16[512,3,128]{2,0,1:T(8,128)(2,1)S(1)}, u32[]{:S(2)}, u32[]{:S(2)}) collective-permute-start(bf16[512,3,128]{2,0,1:T(8,128)(2,1)S(1)} %bitcast.30), channel_id=1, source_target_pairs={{0,16},{8,24},{1,17},{9,25},{2,18},{10,26},{3,19},{11,27},{4,20},{... | collective-permute-start | bytes 1179656 | tf_op jit(solution)/shard_map/ppermute | solution.py:14
  91.1 2.4 %collective-permute-start.3 = (bf16[512,3,128]{2,0,1:T(8,128)(2,1)S(1)}, bf16[512,3,128]{2,0,1:T(8,128)(2,1)S(1)}, u32[]{:S(2)}, u32[]{:S(2)}) collective-permute-start(bf16[512,3,128]{2,0,1:T(8,128)(2,1)S(1)} %bitcast.31), channel_id=1, source_target_pairs={{0,8},{8,16},{16,24},{1,9},{9,17},{17,25},{2,10},{10,18},{18,26},{... | collective-permute-start | bytes 1179656 | tf_op jit(solution)/shard_map/ppermute | solution.py:14
  93.6 1.7 and_and_fusion
  95.3 2.0 collective-permute-start
  97.3 2.7 %collective-permute-start.1 = (bf16[512,3,128]{0,2,1:T(8,128)(2,1)}, bf16[512,3,128]{0,2,1:T(8,128)(2,1)}, u32[]{:S(2)}, u32[]{:S(2)}) collective-permute-start(bf16[512,3,128]{0,2,1:T(8,128)(2,1)} %get-tuple-element.4), channel_id=1, source_target_pairs={{0,8},{8,16},{16,24},{1,9},{9,17},{17,25},{2,10},{10,18},{18,26},{... | collective-permute-start | bytes 1179656 | tf_op jit(solution)/shard_map/ppermute | solution.py:14
  99.9 0.6 collective-permute-done.2
  100.6 8.4 %collective-permute-done.3 = bf16[512,3,128]{2,0,1:T(8,128)(2,1)S(1)} collective-permute-done((bf16[512,3,128]{2,0,1:T(8,128)(2,1)S(1)}, bf16[512,3,128]{2,0,1:T(8,128)(2,1)S(1)}, u32[]{:S(2)}, u32[]{:S(2)}) %collective-permute-start.3) | collective-permute-done | bytes 393248 | tf_op jit(solution)/shard_map/ppermute | solution.py:14
  109.0 2.4 %fusion.21 = f32[3,512,1536]{2,1,0:T(8,128)S(1)} fusion(bf16[512,3,128]{2,0,1:T(8,128)(2,1)S(1)} %bitcast.32, bf16[512,3,128]{2,0,1:T(8,128)(2,1)S(1)} %collective-permute-done.3, bf16[512,3,128]{2,0,1:T(8,128)(2,1)S(1)} %collective-permute-done.2, bf16[512,3,3,128]{0,3,2,1:T(8,128)(2,1)} %bitcast.29), kind=kOutput, calls=%fused_computation.28 | convolution fusion | flops 607518720 | bytes 11010048 | tf_op jit(solution)/shard_map/ihd,jhd->hij/dot_general | solution.py:64
  111.4 9.4 %fusion.39 = (f32[3,512]{1,0:T(4,128)S(1)}, f32[3,512,1536]{2,1,0:T(8,128)}) fusion(f32[3,512,1536]{2,1,0:T(8,128)S(1)} %fusion.21, pred[512,1536]{1,0:T(8,128)(4,1)} %and_and_fusion), kind=kOutput, calls=%fused_computation.63 | output fusion | flops 14157311 | bytes 19666944 | tf_op jit(solution)/shard_map/sub | solution.py:76
  120.8 0.0 collective-permute-done
  120.8 3.9 %collective-permute-done.1 = bf16[512,3,128]{0,2,1:T(8,128)(2,1)} collective-permute-done((bf16[512,3,128]{0,2,1:T(8,128)(2,1)}, bf16[512,3,128]{0,2,1:T(8,128)(2,1)}, u32[]{:S(2)}, u32[]{:S(2)}) %collective-permute-start.1) | collective-permute-done | bytes 393248 | tf_op jit(solution)/shard_map/ppermute | solution.py:14
  124.8 5.8 %fusion.15 = f32[3,128,512]{2,1,0:T(8,128)S(1)} fusion(f32[3,512,1536]{2,1,0:T(8,128)} %get-tuple-element.7, f32[3,512]{1,0:T(4,128)S(1)} %get-tuple-element.6, bf16[512,3,128]{0,2,1:T(8,128)(2,1)} %get-tuple-element.4, bf16[512,3,128]{0,2,1:T(8,128)(2,1)} %collective-permute-done.1, bf16[512,3,128]{0,2,1:T(8,128)(2,1)} %collective-permute-done), kind=kOutput, calls=%fused_computation.22 | convolution fusion | flops 612630528 | bytes 11409408 | tf_op jit(solution)/shard_map/hij,jhd->ihd/dot_general | solution.py:78
  130.6 0.3 copy.35
  130.9 1.2 add_convert_fusion
  132.1 0.0 copy-start.2
  132.1 0.9 gather_fusion
  133.0 1.0 convolution_convert_fusion.1
  133.9 20.8 %all-to-all-start = ((bf16[4,64,384]{2,1,0:T(8,128)(2,1)}), bf16[4,64,384]{2,1,0:T(8,128)(2,1)S(1)}, u32[]{:S(2)}, u32[]{:S(2)}) async-start(bf16[4,64,384]{2,1,0:T(8,128)(2,1)} %bitcast.8), calls=%async_computation | async-start | bytes 393216 | tf_op jit(solution)/shard_map/all_to_all | solution.py:100
  154.8 3.0 %copy.37 = bf16[384,3072]{0,1:T(8,128)(2,1)S(1)} copy(bf16[384,3072]{1,0:T(8,128)(2,1)} %param.10) | data formatting | bytes 4718592 | tf_op args[3]
  157.8 0.0 copy-done.2
  157.8 2.6 %copy.38 = bf16[384,4,768]{2,0,1:T(8,128)(2,1)} copy(bf16[384,4,768]{0,2,1:T(8,128)(2,1)S(1)} %bitcast.27) | data formatting | bytes 4718592 | tf_op jit(solution)/shard_map/all_to_all | solution.py:20
  160.4 1.7 all-to-all-done
  162.1 3.6 %all-to-all-start.1 = ((bf16[384,4,768]{2,0,1:T(8,128)(2,1)}), bf16[384,4,768]{2,0,1:T(8,128)(2,1)S(1)}, u32[]{:S(2)}, u32[]{:S(2)}) async-start(bf16[384,4,768]{2,0,1:T(8,128)(2,1)} %copy.38), calls=%async_computation.1 | async-start | bytes 4718592 | tf_op jit(solution)/shard_map/all_to_all | solution.py:20
  165.7 35.5 %all_gather.7 = bf16[256,1536]{1,0:T(8,128)(2,1)S(1)} all-gather(bf16[256,384]{1,0:T(8,128)(2,1)S(1)} %bitcast.35), channel_id=1, replica_groups=mesh['seq'=4,'phase'=4,'dp'=2] {'phase'}, dimensions={1}, use_global_device_ids=true | all-gather | bytes 983040 | tf_op jit(solution)/shard_map/all_gather | solution.py:19
  201.2 1.2 copy.36
  202.4 0.0 all-to-all-done.1
  202.4 2.2 %convert_reduce_fusion = f32[256,768]{1,0:T(8,128)S(1)} fusion(bf16[256,4,384]{0,2,1:T(8,128)(2,1)} %bitcast.33, bf16[384,4,768]{2,0,1:T(8,128)(2,1)S(1)} %all-to-all-done.1), kind=kOutput, calls=%fused_computation.10 | convolution fusion | flops 606142464 | bytes 3932160 | tf_op jit(solution)/shard_map/nsg,sgc->snc/dot_general | solution.py:24
  204.6 0.1 multiply_reduce_fusion.1
  204.7 8.2 %psum.7 = f32[256]{0:T(256)S(1)} all-reduce(f32[256]{0:T(256)S(1)} %multiply_reduce_fusion.1), channel_id=1, replica_groups=mesh['seq'=4,'phase'=4,'dp'=2] {'phase'}, use_global_device_ids=true, to_apply=%region_6.7 | all-reduce | flops 256 | bytes 2048 | tf_op jit(solution)/shard_map/psum | solution.py:31
  212.9 0.9 multiply_convert_fusion.2
  (13 shorter events, 0.1 us)
Async XLA Ops:
  7.2 2.5 %copy-start = (bf16[512,1536]{1,0:T(8,128)(2,1)S(1)}, bf16[512,1536]{1,0:T(8,128)(2,1)}, u32[]{:S(2)}) copy-start(bf16[512,1536]{1,0:T(8,128)(2,1)} %param.7) | copy-start | bytes 4718596
  7.2 75.0 %all-gather.2.cloned.1.call-start = ((), (), s32[]{:S(2)}) async-start(), calls=%async_computation.2 | async-start | bytes 4423680 | tf_op jit(solution)/shard_map/all_gather | solution.py:47
  9.6 2.1 copy-start.4
  9.6 2.1 copy-start.6
  9.7 72.5 %copy-start.5 = (f32[1536]{0:T(1024)S(1)}, f32[1536]{0:T(1024)}, u32[]{:S(2)}) copy-start(f32[1536]{0:T(1024)} %param.8) | copy-start | bytes 18436
  87.1 13.5 %copy-start.1 = (bf16[512,1152]{0,1:T(8,128)(2,1)}, bf16[512,1152]{0,1:T(8,128)(2,1)S(1)}, u32[]{:S(2)}) copy-start(bf16[512,1152]{0,1:T(8,128)(2,1)S(1)} %copy.32) | copy-start | bytes 3538948
  88.2 12.4 %collective-permute-start.2 = (bf16[512,3,128]{2,0,1:T(8,128)(2,1)S(1)}, bf16[512,3,128]{2,0,1:T(8,128)(2,1)S(1)}, u32[]{:S(2)}, u32[]{:S(2)}) collective-permute-start(bf16[512,3,128]{2,0,1:T(8,128)(2,1)S(1)} %bitcast.30), channel_id=1, source_target_pairs={{0,16},{8,24},{1,17},{9,25},{2,18},{10,26},{3,19},{11,27},{4,20},{... | collective-permute-start | bytes 1179656 | tf_op jit(solution)/shard_map/ppermute | solution.py:14
  91.1 17.9 %collective-permute-start.3 = (bf16[512,3,128]{2,0,1:T(8,128)(2,1)S(1)}, bf16[512,3,128]{2,0,1:T(8,128)(2,1)S(1)}, u32[]{:S(2)}, u32[]{:S(2)}) collective-permute-start(bf16[512,3,128]{2,0,1:T(8,128)(2,1)S(1)} %bitcast.31), channel_id=1, source_target_pairs={{0,8},{8,16},{16,24},{1,9},{9,17},{17,25},{2,10},{10,18},{18,26},{... | collective-permute-start | bytes 1179656 | tf_op jit(solution)/shard_map/ppermute | solution.py:14
  95.3 25.6 %collective-permute-start = (bf16[512,3,128]{0,2,1:T(8,128)(2,1)}, bf16[512,3,128]{0,2,1:T(8,128)(2,1)}, u32[]{:S(2)}, u32[]{:S(2)}) collective-permute-start(bf16[512,3,128]{0,2,1:T(8,128)(2,1)} %get-tuple-element.4), channel_id=1, source_target_pairs={{0,16},{8,24},{1,17},{9,25},{2,18},{10,26},{3,19},{11,27},{4,20},{... | collective-permute-start | bytes 1179656 | tf_op jit(solution)/shard_map/ppermute | solution.py:14
  97.3 27.5 %collective-permute-start.1 = (bf16[512,3,128]{0,2,1:T(8,128)(2,1)}, bf16[512,3,128]{0,2,1:T(8,128)(2,1)}, u32[]{:S(2)}, u32[]{:S(2)}) collective-permute-start(bf16[512,3,128]{0,2,1:T(8,128)(2,1)} %get-tuple-element.4), channel_id=1, source_target_pairs={{0,8},{8,16},{16,24},{1,9},{9,17},{17,25},{2,10},{10,18},{18,26},{... | collective-permute-start | bytes 1179656 | tf_op jit(solution)/shard_map/ppermute | solution.py:14
  132.1 25.7 %copy-start.2 = (bf16[512,384]{1,0:T(8,128)(2,1)}, bf16[512,384]{1,0:T(8,128)(2,1)S(1)}, u32[]{:S(2)}) copy-start(bf16[512,384]{1,0:T(8,128)(2,1)S(1)} %add_convert_fusion) | copy-start | bytes 1179652
  133.9 28.1 %all-to-all-start = ((bf16[4,64,384]{2,1,0:T(8,128)(2,1)}), bf16[4,64,384]{2,1,0:T(8,128)(2,1)S(1)}, u32[]{:S(2)}, u32[]{:S(2)}) async-start(bf16[4,64,384]{2,1,0:T(8,128)(2,1)} %bitcast.8), calls=%async_computation | async-start | bytes 393216 | tf_op jit(solution)/shard_map/all_to_all | solution.py:100
  162.1 40.3 %all-to-all-start.1 = ((bf16[384,4,768]{2,0,1:T(8,128)(2,1)}), bf16[384,4,768]{2,0,1:T(8,128)(2,1)S(1)}, u32[]{:S(2)}, u32[]{:S(2)}) async-start(bf16[384,4,768]{2,0,1:T(8,128)(2,1)} %copy.38), calls=%async_computation.1 | async-start | bytes 4718592 | tf_op jit(solution)/shard_map/all_to_all | solution.py:20
  202.4 10.6 %copy-start.3 = (f32[768]{0:T(1024)S(1)}, f32[768]{0:T(1024)}, u32[]{:S(2)}) copy-start(f32[768]{0:T(1024)} %param.11) | copy-start | bytes 9220
Sparse Core Ops, SparseCore 0:
  9.7 72.4 all-gather.1
where the time goes:
time: 221 us
  waiting for transfers between devices  84.5 us (38%)
  blocking collectives  43.7 us (20%)
  starting transfers between devices  34.5 us (16%)
  other arithmetic  16 us (7%)
  matrix products  15.7 us (7%)
  between operations  14.3 us (6%)
  local copies, waits for them, and re-layouts  12 us (5%)
    all_gather x1, waiting for transfers between devices, on_device(): piece = lax.all_gather(w_qkv, 'seq', axis=0, tiled=True)  69.8 us
    all_gather x1, blocking collectives, project_rows(): full_rows = lax.all_gather(rows, 'phase', axis=1, tiled=True)  35.5 us
    all_to_all x1, starting transfers between devices, on_device(): lax.all_to_all(outgoing, 'seq', split_axis=0, concat_axis=0, tiled=True)  20.8 us
    ppermute x4, waiting for transfers between devices, passed_along(): return lax.ppermute(value, axis, pairs)  13 us
    ppermute x4, starting transfers between devices, passed_along(): return lax.ppermute(value, axis, pairs)  10 us
    sub x1, other arithmetic, on_device(): expo = jnp.exp(scores - top)  9.4 us
    psum x1, blocking collectives, project_rows(): squares = lax.psum(jnp.sum(projected * projected, axis=1), 'phase')  8.2 us
    dot_general x1, matrix products, on_device(): jnp.einsum('hij,jhd->ihd', probs, value_all, preferred_element_type=jnp.f...  5.83 us
  transfers between devices with their start and end apart: 7, of which 5 were waited for; matrix products, arithmetic and copies ran while one was open for 10% of the time, Pallas kernels for 0%

commit v1 on v0

--- a/solution.py
+++ b/solution.py
@@ -1,3 +1,4 @@
+import functools
 import jax
 import jax.numpy as jnp
 from jax import lax
@@ -6,6 +7,27 @@
 DC = 3072
 HD = 128
 WINDOW = 1024
+
+
+def tell_slices_on(load, across, out_dim, k_dim):
+    piece_next = lax.axis_size(across)
+    v1 = lax.axis_index(across)
+    opened, part_now = (piece_next, v1)
+    built = load.shape[out_dim] // opened
+    work_now = jnp.roll(load, -part_now * built, axis=out_dim)
+    new = lax.slice_in_dim(work_now, 0, built, axis=out_dim)
+    pile = [new]
+    for k0 in range(1, opened):
+        latest = lax.slice_in_dim(work_now, k0 * built, (k0 + 1) * built, axis=out_dim)
+        t_next = lax.ppermute(
+            latest, across, perm=[(jj, (jj + k0) % opened) for jj in range(opened)]
+        )
+        pile.append(t_next)
+    w_next = jnp.concatenate(pile[::-1], axis=k_dim)
+    return jnp.roll(w_next, (part_now + 1) * pile[0].shape[k_dim], axis=k_dim)
+
+
+_play_edge = functools.partial(tell_slices_on, across="seq", out_dim=0, k_dim=0)
 
 
 def passed_along(value, axis, by):
@@ -97,9 +119,7 @@
         jnp.bfloat16
     )
     outgoing = outgoing.reshape(n_seq, slot_count, width_dev)
-    arrived = lax.all_to_all(outgoing, "seq", split_axis=0, concat_axis=0, tiled=True).reshape(
-        n_seq * slot_count, width_dev
-    )
+    arrived = _play_edge(outgoing).reshape(n_seq * slot_count, width_dev)
     stretch_states = project_rows(arrived, w_up, out_gain)
     return (byte_states, stretch_states)
 

time: 221 us -> 193 us (0.87)
  blocking collectives: 43.7 us -> 22.3 us
  waiting for transfers between devices: 84.5 us -> 76.3 us
  starting transfers between devices: 34.5 us -> 36.9 us
    all_gather x1, blocking collectives: 35.5 us -> 13.4 us  [project_rows(): full_rows = lax.all_gather(rows, 'phase', axis=1, tiled=True)]
    ppermute x0 -> x3, starting transfers between devices: none -> 22.1 us  [tell_slices_on(): lax.ppermute(latest, across, perm=[(jj, (jj + k0) % opened) for jj in ran...]
    all_to_all x1 -> x0, starting transfers between devices: 20.8 us -> none  [on_device(): lax.all_to_all(outgoing, 'seq', split_axis=0, concat_axis=0, tiled=True)]
    all_gather x1, waiting for transfers between devices: 69.8 us -> 58.9 us  [on_device(): piece = lax.all_gather(w_qkv, 'seq', axis=0, tiled=True)]
    ppermute x0 -> x3, waiting for transfers between devices: none -> 5.25 us  [tell_slices_on(): lax.ppermute(latest, across, perm=[(jj, (jj + k0) % opened) for jj in ran...]
  transfers between devices with their start and end apart: 7 -> 9, of which waited for: 5 -> 6; matrix products, arithmetic and copies ran while one was open for 10% -> 19% of each run, Pallas kernels for 0% -> 0%
where the time goes in v1:
time: 193 us
  waiting for transfers between devices  76.3 us (40%)
  starting transfers between devices  36.9 us (19%)
  blocking collectives  22.3 us (12%)
  other arithmetic  16.4 us (8%)
  matrix products  15.5 us (8%)
  between operations  14.3 us (7%)
  local copies, waits for them, and re-layouts  11.1 us (6%)
    all_gather x1, waiting for transfers between devices, on_device(): piece = lax.all_gather(w_qkv, 'seq', axis=0, tiled=True)  58.9 us
    ppermute x3, starting transfers between devices, tell_slices_on(): lax.ppermute(latest, across, perm=[(jj, (jj + k0) % opened) for jj in ran...  22.1 us
    all_gather x1, blocking collectives, project_rows(): full_rows = lax.all_gather(rows, 'phase', axis=1, tiled=True)  13.4 us
    ppermute x4, waiting for transfers between devices, passed_along(): return lax.ppermute(value, axis, pairs)  12.2 us
    sub x1, other arithmetic, on_device(): expo = jnp.exp(scores - top)  9.51 us
    ppermute x4, starting transfers between devices, passed_along(): return lax.ppermute(value, axis, pairs)  9.44 us
    psum x1, blocking collectives, project_rows(): squares = lax.psum(jnp.sum(projected * projected, axis=1), 'phase')  8.91 us
    dot_general x1, matrix products, on_device(): jnp.einsum('hij,jhd->ihd', probs, value_all, preferred_element_type=jnp.f...  5.83 us
  transfers between devices with their start and end apart: 9, of which 6 were waited for; matrix products, arithmetic and copies ran while one was open for 19% of the time, Pallas kernels for 0%

profile of v1, /device:TPU:0, one launch (start us, length us, event | category | flops | bytes accessed | tf_op | source)
XLA Modules:
  0.0 192.9 jit_solution(7715281674371067789)
XLA Ops:
  7.2 0.0 all-gather.2.cloned.1.call-start
  7.2 2.3 %copy.31 = bf16[384,3,384]{0,2,1:T(8,128)(2,1)} copy(bf16[384,3,384]{2,0,1:T(8,128)(2,1)} %param.11) | data formatting | bytes 1769472 | tf_op args[2]
  9.5 0.0 all-gather.2.cloned.1.call-update
  9.5 3.0 %copy.37 = bf16[384,3072]{0,1:T(8,128)(2,1)S(1)} copy(bf16[384,3072]{1,0:T(8,128)(2,1)} %param.12) | data formatting | bytes 4718592 | tf_op args[3]
  12.5 2.6 %copy.38 = bf16[384,4,768]{2,0,1:T(8,128)(2,1)} copy(bf16[384,4,768]{0,2,1:T(8,128)(2,1)S(1)} %bitcast.27) | data formatting | bytes 4718592 | tf_op jit(solution)/shard_map/all_to_all | solution.py:42
  15.1 5.3 %all-to-all-start = ((bf16[384,4,768]{2,0,1:T(8,128)(2,1)}), bf16[384,4,768]{2,0,1:T(8,128)(2,1)}, u32[]{:S(2)}, u32[]{:S(2)}) async-start(bf16[384,4,768]{2,0,1:T(8,128)(2,1)} %copy.38), calls=%async_computation | async-start | bytes 4718592 | tf_op jit(solution)/shard_map/all_to_all | solution.py:42
  20.5 0.0 copy-start.5
  20.5 2.0 %convert_element_type.44 = f32[512,1536]{1,0:T(8,128)} convert(bf16[512,1536]{1,0:T(8,128)(2,1)S(1)} %copy-done) | non-fusion elementwise | flops 786432 | bytes 4718592 | tf_op jit(solution)/shard_map/convert_element_type | solution.py:65
  22.6 0.2 convert_reduce_fusion.1
  22.8 0.4 multiply_reduce_fusion
  23.2 58.9 %all-gather.2.cloned.1.call-done = bf16[1536,3,384]{0,2,1:T(8,128)(2,1)} async-done(((bf16[384,3,384]{0,2,1:T(8,128)(2,1)}), bf16[1536,3,384]{0,2,1:T(8,128)(2,1)}) %all-gather.2.cloned.1.call-update) | async-done | bytes 3538960 | tf_op jit(solution)/shard_map/all_gather | solution.py:69
  82.1 4.2 %convolution_convert_fusion = bf16[512,1152]{1,0:T(8,128)(2,1)S(1)} fusion(bf16[1536,1152]{0,1:T(8,128)(2,1)} %bitcast.37, f32[1536]{0:T(1024)S(1)} %copy-done.5, f32[512]{0:T(512)S(1)} %add_rsqrt_fusion, bf16[512,1536]{1,0:T(8,128)(2,1)S(1)} %copy-done), kind=kOutput, calls=%fused_computation.14 | convolution fusion | flops 1815674880 | bytes 6299648 | tf_op jit(solution)/shard_map/dot_general | solution.py:70
  86.4 0.6 copy.32
  87.0 0.9 slice_bitcast_fusion.2
  87.9 0.2 copy.42
  88.1 1.7 collective-permute-start.3
  89.8 3.6 %collective-permute-start.2 = (bf16[512,3,128]{2,0,1:T(8,128)(2,1)S(1)}, bf16[512,3,128]{2,0,1:T(8,128)(2,1)S(1)}, u32[]{:S(2)}, u32[]{:S(2)}) collective-permute-start(bf16[512,3,128]{2,0,1:T(8,128)(2,1)S(1)} %bitcast.31), channel_id=1, source_target_pairs={{0,16},{8,24},{1,17},{9,25},{2,18},{10,26},{3,19},{11,27},{4,20},{... | collective-permute-start | bytes 1179656 | tf_op jit(solution)/shard_map/ppermute | solution.py:36
  93.5 1.7 and_and_fusion
  95.2 2.1 %collective-permute-start.1 = (bf16[512,3,128]{0,2,1:T(8,128)(2,1)}, bf16[512,3,128]{0,2,1:T(8,128)(2,1)}, u32[]{:S(2)}, u32[]{:S(2)}) collective-permute-start(bf16[512,3,128]{0,2,1:T(8,128)(2,1)} %get-tuple-element.5), channel_id=1, source_target_pairs={{0,8},{8,16},{16,24},{1,9},{9,17},{17,25},{2,10},{10,18},{18,26},{... | collective-permute-start | bytes 1179656 | tf_op jit(solution)/shard_map/ppermute | solution.py:36
  97.3 2.0 %collective-permute-start = (bf16[512,3,128]{0,2,1:T(8,128)(2,1)}, bf16[512,3,128]{0,2,1:T(8,128)(2,1)}, u32[]{:S(2)}, u32[]{:S(2)}) collective-permute-start(bf16[512,3,128]{0,2,1:T(8,128)(2,1)} %get-tuple-element.5), channel_id=1, source_target_pairs={{0,16},{8,24},{1,17},{9,25},{2,18},{10,26},{3,19},{11,27},{4,20},{... | collective-permute-start | bytes 1179656 | tf_op jit(solution)/shard_map/ppermute | solution.py:36
  99.3 0.0 collective-permute-done.3
  99.3 8.5 %collective-permute-done.2 = bf16[512,3,128]{2,0,1:T(8,128)(2,1)S(1)} collective-permute-done((bf16[512,3,128]{2,0,1:T(8,128)(2,1)S(1)}, bf16[512,3,128]{2,0,1:T(8,128)(2,1)S(1)}, u32[]{:S(2)}, u32[]{:S(2)}) %collective-permute-start.2) | collective-permute-done | bytes 393248 | tf_op jit(solution)/shard_map/ppermute | solution.py:36
  107.8 2.4 %fusion.21 = f32[3,512,1536]{2,1,0:T(8,128)S(1)} fusion(bf16[512,3,128]{2,0,1:T(8,128)(2,1)S(1)} %bitcast.32, bf16[512,3,128]{2,0,1:T(8,128)(2,1)S(1)} %collective-permute-done.3, bf16[512,3,128]{2,0,1:T(8,128)(2,1)S(1)} %collective-permute-done.2, bf16[512,3,3,128]{0,3,2,1:T(8,128)(2,1)} %bitcast.29), kind=kOutput, calls=%fused_computation.28 | convolution fusion | flops 607518720 | bytes 11010048 | tf_op jit(solution)/shard_map/ihd,jhd->hij/dot_general | solution.py:86
  110.2 9.5 %fusion.48 = (f32[3,512]{1,0:T(4,128)S(1)}, f32[3,512,1536]{2,1,0:T(8,128)}) fusion(f32[3,512,1536]{2,1,0:T(8,128)S(1)} %fusion.21, pred[512,1536]{1,0:T(8,128)(4,1)} %and_and_fusion), kind=kOutput, calls=%fused_computation.82 | output fusion | flops 14157311 | bytes 19666944 | tf_op jit(solution)/shard_map/sub | solution.py:98
  119.7 0.0 collective-permute-done.1
  119.7 3.7 %collective-permute-done = bf16[512,3,128]{0,2,1:T(8,128)(2,1)} collective-permute-done((bf16[512,3,128]{0,2,1:T(8,128)(2,1)}, bf16[512,3,128]{0,2,1:T(8,128)(2,1)}, u32[]{:S(2)}, u32[]{:S(2)}) %collective-permute-start) | collective-permute-done | bytes 393248 | tf_op jit(solution)/shard_map/ppermute | solution.py:36
  123.4 5.8 %fusion.15 = f32[3,128,512]{2,1,0:T(8,128)S(1)} fusion(f32[3,512,1536]{2,1,0:T(8,128)} %get-tuple-element.12, f32[3,512]{1,0:T(4,128)S(1)} %get-tuple-element.11, bf16[512,3,128]{0,2,1:T(8,128)(2,1)} %get-tuple-element.5, bf16[512,3,128]{0,2,1:T(8,128)(2,1)} %collective-permute-done.1, bf16[512,3,128]{0,2,1:T(8,128)(2,1)} %collective-permute-done), kind=kOutput, calls=%fused_computation.22 | convolution fusion | flops 612630528 | bytes 11409408 | tf_op jit(solution)/shard_map/hij,jhd->ihd/dot_general | solution.py:100
  129.2 0.3 copy.35
  129.5 1.2 add_convert_fusion
  130.7 0.0 copy-start.2
  130.7 0.9 gather_fusion
  131.6 0.3 convolution_convert_fusion.1
  131.9 0.1 fusion.36
  132.0 21.5 %collective-permute-start.4 = (bf16[1,64,384]{2,1,0:T(8,128)(2,1)S(1)}, bf16[1,64,384]{2,1,0:T(8,128)(2,1)S(1)}, u32[]{:S(2)}, u32[]{:S(2)}) collective-permute-start(bf16[1,64,384]{2,1,0:T(8,128)(2,1)S(1)} %get-tuple-element.10), channel_id=1, source_target_pairs={{0,24},{8,0},{16,8},{24,16},{1,25},{9,1},{17,9},{25,17},{2,26},{10... | collective-permute-start | bytes 147464 | tf_op jit(solution)/shard_map/ppermute | solution.py:22
  153.5 0.0 collective-permute-start.5
  153.5 0.6 collective-permute-start.6
  154.2 1.1 collective-permute-done.4
  155.3 3.2 %collective-permute-done.5 = bf16[1,64,384]{2,1,0:T(8,128)(2,1)S(1)} collective-permute-done((bf16[1,64,384]{2,1,0:T(8,128)(2,1)S(1)}, bf16[1,64,384]{2,1,0:T(8,128)(2,1)S(1)}, u32[]{:S(2)}, u32[]{:S(2)}) %collective-permute-start.5) | collective-permute-done | bytes 49184 | tf_op jit(solution)/shard_map/ppermute | solution.py:22
  158.5 0.9 collective-permute-done.6
  159.4 0.2 fusion.32
  159.6 13.4 %all_gather.7 = bf16[256,1536]{1,0:T(8,128)(2,1)S(1)} all-gather(bf16[256,384]{1,0:T(8,128)(2,1)S(1)} %bitcast.36), channel_id=1, replica_groups=mesh['seq'=4,'phase'=4,'dp'=2] {'phase'}, dimensions={1}, use_global_device_ids=true | all-gather | bytes 983040 | tf_op jit(solution)/shard_map/all_gather | solution.py:41
  173.0 0.3 copy.36
  173.3 0.0 all-to-all-done
  173.3 0.0 copy-start.3
  173.3 2.8 %convert_reduce_fusion = f32[256,768]{1,0:T(8,128)S(1)} fusion(bf16[256,4,384]{0,2,1:T(8,128)(2,1)S(1)} %bitcast.33, bf16[384,4,768]{2,0,1:T(8,128)(2,1)} %all-to-all-done), kind=kOutput, calls=%fused_computation.10 | convolution fusion | flops 606142464 | bytes 3932160 | tf_op jit(solution)/shard_map/nsg,sgc->snc/dot_general | solution.py:46
  176.1 0.1 multiply_reduce_fusion.1
  176.2 8.9 %psum.7 = f32[256]{0:T(256)S(1)} all-reduce(f32[256]{0:T(256)S(1)} %multiply_reduce_fusion.1), channel_id=1, replica_groups=mesh['seq'=4,'phase'=4,'dp'=2] {'phase'}, use_global_device_ids=true, to_apply=%region_6.8 | all-reduce | flops 256 | bytes 2048 | tf_op jit(solution)/shard_map/psum | solution.py:53
  185.1 0.9 multiply_convert_fusion.2
  (20 shorter events, 0.1 us)
Async XLA Ops:
  7.2 74.9 %all-gather.2.cloned.1.call-start = ((), (), s32[]{:S(2)}) async-start(), calls=%async_computation.1 | async-start | bytes 4423680 | tf_op jit(solution)/shard_map/all_gather | solution.py:69
  15.1 5.3 %copy-start = (bf16[512,1536]{1,0:T(8,128)(2,1)S(1)}, bf16[512,1536]{1,0:T(8,128)(2,1)}, u32[]{:S(2)}) copy-start(bf16[512,1536]{1,0:T(8,128)(2,1)} %param.9) | copy-start | bytes 4718596
  15.1 158.1 %all-to-all-start = ((bf16[384,4,768]{2,0,1:T(8,128)(2,1)}), bf16[384,4,768]{2,0,1:T(8,128)(2,1)}, u32[]{:S(2)}, u32[]{:S(2)}) async-start(bf16[384,4,768]{2,0,1:T(8,128)(2,1)} %copy.38), calls=%async_computation | async-start | bytes 4718592 | tf_op jit(solution)/shard_map/all_to_all | solution.py:42
  20.5 2.1 %copy-start.4 = (s32[128]{0:T(128)S(1)}, s32[128]{0:T(128)}, u32[]{:S(2)}) copy-start(s32[128]{0:T(128)} %param.14) | copy-start | bytes 1540
  20.5 2.1 %copy-start.6 = (s32[128,1]{0,1:T(1,128)S(1)}, s32[128,1]{0,1:T(1,128)}, u32[]{:S(2)}) copy-start(s32[128,1]{0,1:T(1,128)} %param.15) | copy-start | bytes 1540
  20.5 61.6 %copy-start.5 = (f32[1536]{0:T(1024)S(1)}, f32[1536]{0:T(1024)}, u32[]{:S(2)}) copy-start(f32[1536]{0:T(1024)} %param.10) | copy-start | bytes 18436
  87.0 12.3 %copy-start.1 = (bf16[512,1152]{0,1:T(8,128)(2,1)}, bf16[512,1152]{0,1:T(8,128)(2,1)S(1)}, u32[]{:S(2)}) copy-start(bf16[512,1152]{0,1:T(8,128)(2,1)S(1)} %copy.32) | copy-start | bytes 3538948
  88.1 11.1 %collective-permute-start.3 = (bf16[512,3,128]{2,0,1:T(8,128)(2,1)S(1)}, bf16[512,3,128]{2,0,1:T(8,128)(2,1)S(1)}, u32[]{:S(2)}, u32[]{:S(2)}) collective-permute-start(bf16[512,3,128]{2,0,1:T(8,128)(2,1)S(1)} %bitcast.30), channel_id=1, source_target_pairs={{0,8},{8,16},{16,24},{1,9},{9,17},{17,25},{2,10},{10,18},{18,26},{... | collective-permute-start | bytes 1179656 | tf_op jit(solution)/shard_map/ppermute | solution.py:36
  89.8 17.9 %collective-permute-start.2 = (bf16[512,3,128]{2,0,1:T(8,128)(2,1)S(1)}, bf16[512,3,128]{2,0,1:T(8,128)(2,1)S(1)}, u32[]{:S(2)}, u32[]{:S(2)}) collective-permute-start(bf16[512,3,128]{2,0,1:T(8,128)(2,1)S(1)} %bitcast.31), channel_id=1, source_target_pairs={{0,16},{8,24},{1,17},{9,25},{2,18},{10,26},{3,19},{11,27},{4,20},{... | collective-permute-start | bytes 1179656 | tf_op jit(solution)/shard_map/ppermute | solution.py:36
  95.2 24.5 %collective-permute-start.1 = (bf16[512,3,128]{0,2,1:T(8,128)(2,1)}, bf16[512,3,128]{0,2,1:T(8,128)(2,1)}, u32[]{:S(2)}, u32[]{:S(2)}) collective-permute-start(bf16[512,3,128]{0,2,1:T(8,128)(2,1)} %get-tuple-element.5), channel_id=1, source_target_pairs={{0,8},{8,16},{16,24},{1,9},{9,17},{17,25},{2,10},{10,18},{18,26},{... | collective-permute-start | bytes 1179656 | tf_op jit(solution)/shard_map/ppermute | solution.py:36
  97.3 26.2 %collective-permute-start = (bf16[512,3,128]{0,2,1:T(8,128)(2,1)}, bf16[512,3,128]{0,2,1:T(8,128)(2,1)}, u32[]{:S(2)}, u32[]{:S(2)}) collective-permute-start(bf16[512,3,128]{0,2,1:T(8,128)(2,1)} %get-tuple-element.5), channel_id=1, source_target_pairs={{0,16},{8,24},{1,17},{9,25},{2,18},{10,26},{3,19},{11,27},{4,20},{... | collective-permute-start | bytes 1179656 | tf_op jit(solution)/shard_map/ppermute | solution.py:36
  130.7 42.5 %copy-start.2 = (bf16[512,384]{1,0:T(8,128)(2,1)}, bf16[512,384]{1,0:T(8,128)(2,1)S(1)}, u32[]{:S(2)}) copy-start(bf16[512,384]{1,0:T(8,128)(2,1)S(1)} %add_convert_fusion) | copy-start | bytes 1179652
  132.0 23.2 %collective-permute-start.4 = (bf16[1,64,384]{2,1,0:T(8,128)(2,1)S(1)}, bf16[1,64,384]{2,1,0:T(8,128)(2,1)S(1)}, u32[]{:S(2)}, u32[]{:S(2)}) collective-permute-start(bf16[1,64,384]{2,1,0:T(8,128)(2,1)S(1)} %get-tuple-element.10), channel_id=1, source_target_pairs={{0,24},{8,0},{16,8},{24,16},{1,25},{9,1},{17,9},{25,17},{2,26},{10... | collective-permute-start | bytes 147464 | tf_op jit(solution)/shard_map/ppermute | solution.py:22
  153.5 5.0 %collective-permute-start.5 = (bf16[1,64,384]{2,1,0:T(8,128)(2,1)S(1)}, bf16[1,64,384]{2,1,0:T(8,128)(2,1)S(1)}, u32[]{:S(2)}, u32[]{:S(2)}) collective-permute-start(bf16[1,64,384]{2,1,0:T(8,128)(2,1)S(1)} %get-tuple-element.9), channel_id=1, source_target_pairs={{0,16},{8,24},{16,0},{24,8},{1,17},{9,25},{17,1},{25,9},{2,18},{10... | collective-permute-start | bytes 147464 | tf_op jit(solution)/shard_map/ppermute | solution.py:22
  153.5 5.9 %collective-permute-start.6 = (bf16[1,64,384]{2,1,0:T(8,128)(2,1)S(1)}, bf16[1,64,384]{2,1,0:T(8,128)(2,1)S(1)}, u32[]{:S(2)}, u32[]{:S(2)}) collective-permute-start(bf16[1,64,384]{2,1,0:T(8,128)(2,1)S(1)} %get-tuple-element.8), channel_id=1, source_target_pairs={{0,8},{8,16},{16,24},{24,0},{1,9},{9,17},{17,25},{25,1},{2,10},{10... | collective-permute-start | bytes 147464 | tf_op jit(solution)/shard_map/ppermute | solution.py:22
  173.3 11.8 %copy-start.3 = (f32[768]{0:T(1024)S(1)}, f32[768]{0:T(1024)}, u32[]{:S(2)}) copy-start(f32[768]{0:T(1024)} %param.13) | copy-start | bytes 9220
Sparse Core Ops, SparseCore 0:
  9.6 72.4 all-gather.1
